TPU v7x, 32 devices: a whole 2x2x4 slice. The times are simulated.
32 devices in a mesh: strip: 4 (over z), mr: 8 (over y, x, core).
Axes of the slice: x: 2, y: 2, z: 4, core: 2. Of those that a mesh axis runs over, the one named last changes fastest.
Arguments:
- alm: bfloat16 [2, 256, 2048], P(None, ('strip', 'mr')), may hold values from -6 to 6
- beam: float32 [13, 2048], replicated, may hold values from -6 to 6
- wigner: bfloat16 [256, 13, 32, 2048], P(('strip', 'mr')), may hold values from -0.125 to 0.125
- base_index: int32 [8192], P(('strip', 'mr')), may hold values from 0 to 16124
- interp_weights: float32 [12, 8192], P(None, ('strip', 'mr')), may hold values from -3 to 3
- live_counts: int32 [32, 32], P(('strip', 'mr')), may hold values from 0 to 8, as said below
Outputs:
- tod: float32 [8192], P(('strip', 'mr'))
Inputs may be any that keep to these rules, and one draw needn't show every extreme that they name: live_counts[i, d] counts the used slots from device i to block d; blocks differ in how many samples point into them, and some pair uses all 8 slots in every draw.
All inputs are finite; a program needn't handle non-finite values.
Results may differ from a plain program's by a relative error of at most 0.0055.
Values may be sent and summed in bfloat16 or wider, within the bound.
No kernel may reach another device: no remote copies, remote signals or barrier semaphores. Data moves between devices by JAX's collectives and lax.ppermute only.
A program may use at most 64 MiB of HBM per device.

v0:
```python
import math
import jax
import jax.numpy as jnp
from jax import lax
from jax.sharding import PartitionSpec as P


def padded_2(x, sides, width):
    for axis, dim in sides:
        devices, length = (lax.axis_size(axis), x.shape[dim])
        up = [(i, (i + 1) % devices) for i in range(devices)]
        down = [(j, i) for i, j in up]
        last = lax.slice_in_dim(x, length - width, length, axis=dim)
        first = lax.slice_in_dim(x, 0, width, axis=dim)
        before = lax.ppermute(last, axis, up)
        after = lax.ppermute(first, axis, down)
        x = jnp.concatenate([before, x, after], axis=dim)
    return x


def phase_tables(m_first, m_count, phi_count, phi_total):
    m_vals = m_first + jnp.arange(m_count, dtype=jnp.int32)
    phi_vals = jnp.arange(phi_count, dtype=jnp.int32)
    product = phi_vals[:, None] * m_vals[None, :] % phi_total
    angle = 2.0 * math.pi / phi_total * product.astype(jnp.float32)
    return (jnp.cos(angle).astype(jnp.bfloat16), jnp.sin(angle).astype(jnp.bfloat16))


def orient_table(psi_count, k_count):
    product = (
        jnp.arange(psi_count, dtype=jnp.int32)[:, None]
        * jnp.arange(k_count, dtype=jnp.int32)[None, :]
        % psi_count
    )
    angle = 2.0 * math.pi / psi_count * product.astype(jnp.float32)
    return jnp.stack([jnp.cos(angle), -jnp.sin(angle)], axis=1)


def phi_sum(cos_table, sin_table, coef):
    real_part = jnp.dot(cos_table, coef[0], preferred_element_type=jnp.float32) - jnp.dot(
        sin_table, coef[1], preferred_element_type=jnp.float32
    )
    imag_part = jnp.dot(sin_table, coef[0], preferred_element_type=jnp.float32) + jnp.dot(
        cos_table, coef[1], preferred_element_type=jnp.float32
    )
    return jnp.concatenate([real_part, imag_part], axis=1)


def decode(base, lat_dev, phi_dev):
    phi_base = base % (phi_dev + 1)
    rest = base // (phi_dev + 1)
    return (rest // (lat_dev + 1), rest % (lat_dev + 1), phi_base)


def tap_table(index, tap_weights, length):
    positions = jnp.arange(length, dtype=jnp.int32)[:, None]
    table = jnp.zeros((length, index.shape[1]), jnp.float32)
    for offset in range(4):
        table = table + jnp.where(
            positions == index[offset][None, :], tap_weights[offset][None, :], 0.0
        )
    return table


def stencil(cube_block, psi_idx, lat_idx, phi_idx, weights, lat_weight):
    psi_len, lat_len, phi_len = cube_block.shape
    phi_table = tap_table(phi_idx, weights[4:8], phi_len)
    lat_table = tap_table(lat_idx, lat_weight, lat_len)
    psi_table = tap_table(psi_idx, weights[8:12], psi_len)
    along = jnp.dot(
        cube_block.reshape(psi_len * lat_len, phi_len).astype(jnp.float32),
        phi_table,
        precision=lax.Precision.HIGHEST,
    )
    along = along.reshape(psi_len, lat_len, -1)
    across = jnp.sum(along * lat_table[None], axis=1)
    return jnp.sum(across * psi_table, axis=0)


def owner_values(packet_in, padded, lat_dev, phi_dev, psi_count):
    shape = packet_in.shape[1:]
    flat = packet_in.reshape(packet_in.shape[0], -1)
    psi_base, lat_base, phi_base = decode(flat[12].astype(jnp.int32), lat_dev, phi_dev)
    offs = jnp.arange(4, dtype=jnp.int32)[:, None]
    psi_idx = (psi_base[None] + offs) % psi_count
    lat_idx = lat_base[None] + offs
    phi_idx = phi_base[None] + offs
    return stencil(padded, psi_idx, lat_idx, phi_idx, flat[:12], flat[0:4]).reshape(shape)


def on_device(alm, beam, wigner, base_index, interp_weights, live_counts):
    n_strip = lax.axis_size("strip")
    n_mr = lax.axis_size("mr")
    devices = n_strip * n_mr
    k_count = beam.shape[0]
    mixed = (alm[:, :, None, :].astype(jnp.float32) * beam[None, None, :, :]).astype(jnp.bfloat16)
    coef = jnp.einsum("cmkl,mkrl->cmkr", mixed, wigner, preferred_element_type=jnp.float32).astype(
        jnp.bfloat16
    )
    coef = lax.all_to_all(coef, "mr", split_axis=3, concat_axis=1, tiled=True)
    m_here = coef.shape[1]
    lat_dev = coef.shape[3]
    coef = coef.reshape(2, m_here, k_count * lat_dev)
    m_total = m_here * n_strip
    phi_total = 2 * m_total
    phi_dev = phi_total // n_strip
    strip_at = lax.axis_index("strip")
    m_first = strip_at * m_here
    cos_table, sin_table = phase_tables(
        m_first, m_here, phi_dev * lax.axis_size("strip"), phi_total
    )
    spectra = lax.psum_scatter(
        phi_sum(cos_table, sin_table, coef), "strip", scatter_dimension=0, tiled=True
    )
    spectra = spectra.reshape(phi_dev, 2, k_count, lat_dev)
    psi_count = 2 * k_count - 1
    scale = 1.0 / math.sqrt(m_total * k_count)
    cube = (
        jnp.einsum(
            "pckr,tck->trp",
            spectra,
            orient_table(psi_count, k_count),
            precision=lax.Precision.HIGHEST,
        )
        * scale
    ).astype(jnp.bfloat16)
    cap = base_index.shape[0] // devices
    live = (
        jnp.arange(cap, dtype=jnp.int32)[None, :] < live_counts.reshape(devices)[:, None]
    ).astype(jnp.float32)
    weights = interp_weights.reshape(12, devices, cap)
    lat_w = weights[0:4] * live[None]
    weights = jnp.concatenate([lat_w, weights[4:]], axis=0)
    padded = padded_2(cube, (("strip", 2), ("mr", 1)), 2)
    packet = jnp.concatenate(
        [weights, base_index.reshape(1, devices, cap).astype(jnp.float32)], axis=0
    )
    values = owner_values(
        lax.all_to_all(packet, ("strip", "mr"), split_axis=1, concat_axis=1, tiled=True),
        padded,
        lat_dev,
        phi_dev,
        psi_count,
    )
    result = lax.all_to_all(values, ("strip", "mr"), split_axis=0, concat_axis=0, tiled=True)
    return result.reshape(-1)


def solution(mesh):
    placed = (
        P(None, ("strip", "mr"), None),
        P(),
        P(("strip", "mr"), None, None, None),
        P(("strip", "mr")),
        P(None, ("strip", "mr")),
        P(("strip", "mr"), None),
    )
    return jax.shard_map(
        on_device, mesh=mesh, in_specs=placed, out_specs=P(("strip", "mr")), check_vma=False
    )
```

profile of v0, /device:TPU:0, one launch (start us, length us, event | category | flops | bytes accessed | tf_op | source)
XLA Modules:
  0.0 91.3 jit_solution(9475546606668094492)
XLA Ops:
  6.5 1.0 %copy.40 = f32[2,8,2048]{2,0,1:T(2,128)S(1)} copy(bf16[2,8,2048]{2,1,0:T(8,128)(2,1)} %param.6) | data formatting | bytes 196608 | tf_op jit(solution)/shard_map/convert_element_type | solution.py:96
  7.5 6.8 %fusion.2 = bf16[2,8,13,32]{3,0,2,1:T(2,128)(2,1)S(1)} fusion(bf16[8,13,32,2048]{3,2,1,0:T(8,128)(2,1)} %param.8, f32[13,2048]{1,0:T(8,128)} %param.7, f32[2,8,2048]{2,0,1:T(2,128)S(1)} %copy.40), kind=kOutput, calls=%fused_computation.8 | convolution fusion | flops 28121600 | bytes 13882368 | tf_op jit(solution)/shard_map/cmkl,mkrl->cmkr/dot_general | solution.py:97
  14.4 0.2 copy.41
  14.6 0.8 reshape.386
  15.4 5.2 %all-to-all-start = ((bf16[8,2,416]{2,1,0:T(2,128)(2,1)}), bf16[8,2,416]{2,1,0:T(2,128)(2,1)S(1)}, u32[]{:S(2)}, u32[]{:S(2)}) async-start(bf16[8,2,416]{2,1,0:T(2,128)(2,1)} %reshape.386), calls=%async_computation | async-start | bytes 32768 | tf_op jit(solution)/shard_map/all_to_all | solution.py:100
  21.1 0.9 %copy.46 = f32[13,32,8]{0,2,1:T(8,128)} copy(f32[13,32,8]{2,1,0:T(8,128)S(1)} %pad_maximum_fusion.1) | data formatting | bytes 26624 | tf_op jit(solution)/shard_map/concatenate | solution.py:135
  22.0 3.3 %all-to-all-done = bf16[8,2,416]{2,1,0:T(2,128)(2,1)S(1)} async-done(((bf16[8,2,416]{2,1,0:T(2,128)(2,1)}), bf16[8,2,416]{2,1,0:T(2,128)(2,1)S(1)}, u32[]{:S(2)}, u32[]{:S(2)}) %all-to-all-start) | async-done | bytes 13344 | tf_op jit(solution)/shard_map/all_to_all | solution.py:100
  25.3 4.0 %all-to-all-start.1 = ((f32[13,32,8]{0,2,1:T(8,128)}), f32[13,32,8]{0,2,1:T(8,128)S(1)}, u32[]{:S(2)}, u32[]{:S(2)}) async-start(f32[13,32,8]{0,2,1:T(8,128)} %copy.46), calls=%async_computation.2 | async-start | bytes 262144 | tf_op jit(solution)/shard_map/all_to_all | solution.py:139
  29.3 0.3 reshape.387
  29.7 0.3 copy.43
  30.0 0.1 squeeze.4
  30.1 1.3 %fusion.22 = f32[512,52]{0,1:T(8,128)S(1)} fusion(bf16[64,52]{0,1:T(8,128)(2,1)S(1)} %squeeze.4, s32[64]{0:T(128)S(1)} %iota_add_fusion.2), kind=kOutput, calls=%fused_computation.55 | convolution fusion | flops 3899392 | bytes 113408 | tf_op jit(solution)/shard_map/dot_general | solution.py:43
  31.4 1.3 %fusion.21 = f32[512,52]{0,1:T(8,128)S(1)} fusion(bf16[64,52]{0,1:T(8,128)(2,1)S(1)} %squeeze.4, s32[64]{0:T(128)S(1)} %iota_add_fusion.2), kind=kOutput, calls=%fused_computation.54 | convolution fusion | flops 3899392 | bytes 113408 | tf_op jit(solution)/shard_map/dot_general | solution.py:40
  32.7 0.3 copy.44
  33.1 1.3 %convolution_add_fusion = f32[512,52]{0,1:T(8,128)S(1)} fusion(f32[512,52]{0,1:T(8,128)S(1)} %fusion.22, bf16[64,52]{0,1:T(8,128)(2,1)S(1)} %squeeze.10, s32[64]{0:T(128)S(1)} %iota_add_fusion.2), kind=kOutput, calls=%fused_computation.3 | convolution fusion | flops 3926016 | bytes 219904 | tf_op jit(solution)/shard_map/dot_general | solution.py:43
  34.4 1.3 %convolution_subtract_fusion = f32[512,52]{0,1:T(8,128)S(1)} fusion(f32[512,52]{0,1:T(8,128)S(1)} %fusion.21, bf16[64,52]{0,1:T(8,128)(2,1)S(1)} %squeeze.10, s32[64]{0:T(128)S(1)} %iota_add_fusion.2), kind=kOutput, calls=%fused_computation.4 | convolution fusion | flops 3926016 | bytes 219904 | tf_op jit(solution)/shard_map/dot_general | solution.py:40
  35.8 0.7 pad_maximum_fusion
  36.5 1.0 %all-to-all-done.1 = f32[13,32,8]{0,2,1:T(8,128)S(1)} async-done(((f32[13,32,8]{0,2,1:T(8,128)}), f32[13,32,8]{0,2,1:T(8,128)S(1)}, u32[]{:S(2)}, u32[]{:S(2)}) %all-to-all-start.1) | async-done | bytes 13344 | tf_op jit(solution)/shard_map/all_to_all | solution.py:139
  37.5 0.7 fusion.23
  38.3 1.2 %remainder_reduce_fusion = (s32[32,8]{1,0:T(8,128)S(1)}, s32[32,8]{1,0:T(8,128)S(1)}) fusion(f32[13,32,8]{0,2,1:T(8,128)S(1)} %all-to-all-done.1), kind=kLoop, calls=%fused_computation.53 | loop fusion | flops 768 | bytes 3072 | tf_op jit(solution)/shard_map/jit(remainder)/rem | solution.py:50
  39.8 0.9 slice_reduce_fusion.3
  41.1 16.3 %reduce-scatter.2.cloned.1.call-done = f32[128,104]{0,1:T(8,128)} async-done(((f32[512,104]{0,1:T(8,128)}), f32[128,104]{0,1:T(8,128)}) %reduce-scatter.2.cloned.1.call-update) | async-done | bytes 53264 | tf_op jit(solution)/shard_map/reduce_scatter | solution.py:112
  57.4 1.1 %fusion.4 = bf16[25,4,128]{2,0,1:T(8,128)(2,1)S(1)} fusion(f32[128,2,13,4]{0,3,2,1:T(4,128)} %bitcast.55, f32[25,1,13]{0,2,1:T(8,128)S(1)} %get-tuple-element.40, f32[25,1,13]{0,2,1:T(8,128)S(1)} %get-tuple-element.41), kind=kOutput, calls=%fused_computation.10 | convolution fusion | flops 4019850 | bytes 81448 | tf_op jit(solution)/shard_map/pckr,tck->trp/dot_general | solution.py:119
  58.5 3.8 %collective-permute-start.1 = (bf16[25,4,2]{2,0,1:T(8,128)(2,1)S(1)}, bf16[25,4,2]{2,0,1:T(8,128)(2,1)S(1)}, u32[]{:S(2)}, u32[]{:S(2)}) collective-permute-start(bf16[25,4,2]{2,0,1:T(8,128)(2,1)S(1)} %get-tuple-element.24), channel_id=1, source_target_pairs={{8,0},{16,8},{24,16},{0,24},{9,1},{17,9},{25,17},{1,25},{10,2},{18... | collective-permute-start | bytes 1208 | tf_op jit(solution)/shard_map/ppermute | solution.py:16
  62.4 1.9 %collective-permute-done = bf16[25,4,2]{2,0,1:T(8,128)(2,1)S(1)} collective-permute-done((bf16[25,4,2]{2,0,1:T(8,128)(2,1)S(1)}, bf16[25,4,2]{2,0,1:T(8,128)(2,1)S(1)}, u32[]{:S(2)}, u32[]{:S(2)}) %collective-permute-start) | collective-permute-done | bytes 432 | tf_op jit(solution)/shard_map/ppermute | solution.py:15
  64.4 2.6 %collective-permute-start.3 = (bf16[25,2,132]{2,0,1:T(8,128)(2,1)S(1)}, bf16[25,2,132]{2,0,1:T(8,128)(2,1)S(1)}, u32[]{:S(2)}, u32[]{:S(2)}) collective-permute-start(bf16[25,2,132]{2,0,1:T(8,128)(2,1)S(1)} %get-tuple-element.22), channel_id=1, source_target_pairs={{1,0},{2,1},{3,2},{4,3},{5,4},{6,5},{7,6},{0,7},{9,8},{10,9},{11,1... | collective-permute-start | bytes 39608 | tf_op jit(solution)/shard_map/ppermute | solution.py:16
  67.8 0.9 collective-permute-done.2
  68.8 0.4 fusion
  69.3 13.3 %all_to_all.29 = f32[32,1,8]{2,1,0:T(1,128)S(1)} all-to-all(f32[32,1,8]{2,1,0:T(1,128)S(1)} %bitcast.56), channel_id=1, replica_groups=mesh['strip'=4,'mr'=8] {'strip','mr'}, dimensions={0} | all-to-all | bytes 2048 | tf_op jit(solution)/shard_map/all_to_all | solution.py:145
  82.6 0.5 broadcast.328
  83.1 0.7 reduce.33
  83.8 0.7 reshape.358
  (55 shorter events, 2.5 us)
Async XLA Ops:
  6.5 14.0 %copy-start = (f32[12,256]{1,0:T(8,128)S(1)}, f32[12,256]{1,0:T(8,128)}, u32[]{:S(2)}) copy-start(f32[12,256]{1,0:T(8,128)} %param.10) | copy-start | bytes 36868
  6.5 14.3 %slice-start = ((f32[12,256]{1,0:T(8,128)}), f32[4,256]{1,0:T(4,128)S(1)}, s32[]{:S(2)}) async-start(f32[12,256]{1,0:T(8,128)} %param.10), calls=%async_computation.5 | async-start | bytes 8192 | tf_op jit(solution)/shard_map/slice | solution.py:132
  6.5 14.1 %copy-start.1 = (s32[256]{0:T(256)S(1)}, s32[256]{0:T(256)}, u32[]{:S(2)}) copy-start(s32[256]{0:T(256)} %param.9) | copy-start | bytes 3076
  6.5 14.2 %copy-start.2 = (s32[1,32]{1,0:T(1,128)S(1)}, s32[1,32]{1,0:T(1,128)}, u32[]{:S(2)}) copy-start(s32[1,32]{1,0:T(1,128)} %param.11) | copy-start | bytes 388
  15.4 9.9 %all-to-all-start = ((bf16[8,2,416]{2,1,0:T(2,128)(2,1)}), bf16[8,2,416]{2,1,0:T(2,128)(2,1)S(1)}, u32[]{:S(2)}, u32[]{:S(2)}) async-start(bf16[8,2,416]{2,1,0:T(2,128)(2,1)} %reshape.386), calls=%async_computation | async-start | bytes 32768 | tf_op jit(solution)/shard_map/all_to_all | solution.py:100
  25.3 12.2 %all-to-all-start.1 = ((f32[13,32,8]{0,2,1:T(8,128)}), f32[13,32,8]{0,2,1:T(8,128)S(1)}, u32[]{:S(2)}, u32[]{:S(2)}) async-start(f32[13,32,8]{0,2,1:T(8,128)} %copy.46), calls=%async_computation.2 | async-start | bytes 262144 | tf_op jit(solution)/shard_map/all_to_all | solution.py:139
  29.3 28.1 %reduce-scatter.2.cloned.1.call-start = ((), (), s32[]{:S(2)}) async-start(), calls=%async_computation.4 | async-start | bytes 266240 | tf_op jit(solution)/shard_map/reduce_scatter | solution.py:112
  58.5 5.7 %collective-permute-start = (bf16[25,4,2]{2,0,1:T(8,128)(2,1)S(1)}, bf16[25,4,2]{2,0,1:T(8,128)(2,1)S(1)}, u32[]{:S(2)}, u32[]{:S(2)}) collective-permute-start(bf16[25,4,2]{2,0,1:T(8,128)(2,1)S(1)} %get-tuple-element.23), channel_id=1, source_target_pairs={{0,8},{8,16},{16,24},{24,0},{1,9},{9,17},{17,25},{25,1},{2,10},{10... | collective-permute-start | bytes 1208 | tf_op jit(solution)/shard_map/ppermute | solution.py:15
  58.5 5.7 %collective-permute-start.1 = (bf16[25,4,2]{2,0,1:T(8,128)(2,1)S(1)}, bf16[25,4,2]{2,0,1:T(8,128)(2,1)S(1)}, u32[]{:S(2)}, u32[]{:S(2)}) collective-permute-start(bf16[25,4,2]{2,0,1:T(8,128)(2,1)S(1)} %get-tuple-element.24), channel_id=1, source_target_pairs={{8,0},{16,8},{24,16},{0,24},{9,1},{17,9},{25,17},{1,25},{10,2},{18... | collective-permute-start | bytes 1208 | tf_op jit(solution)/shard_map/ppermute | solution.py:16
  64.4 4.3 %collective-permute-start.2 = (bf16[25,2,132]{2,0,1:T(8,128)(2,1)S(1)}, bf16[25,2,132]{2,0,1:T(8,128)(2,1)S(1)}, u32[]{:S(2)}, u32[]{:S(2)}) collective-permute-start(bf16[25,2,132]{2,0,1:T(8,128)(2,1)S(1)} %get-tuple-element.21), channel_id=1, source_target_pairs={{0,1},{1,2},{2,3},{3,4},{4,5},{5,6},{6,7},{7,0},{8,9},{9,10},{10,1... | collective-permute-start | bytes 39608 | tf_op jit(solution)/shard_map/ppermute | solution.py:15
  64.4 4.2 %collective-permute-start.3 = (bf16[25,2,132]{2,0,1:T(8,128)(2,1)S(1)}, bf16[25,2,132]{2,0,1:T(8,128)(2,1)S(1)}, u32[]{:S(2)}, u32[]{:S(2)}) collective-permute-start(bf16[25,2,132]{2,0,1:T(8,128)(2,1)S(1)} %get-tuple-element.22), channel_id=1, source_target_pairs={{1,0},{2,1},{3,2},{4,3},{5,4},{6,5},{7,6},{0,7},{9,8},{10,9},{11,1... | collective-permute-start | bytes 39608 | tf_op jit(solution)/shard_map/ppermute | solution.py:16
Sparse Core Ops, SparseCore 0:
  36.6 20.7 reduce-scatter.1
where the time goes:
time: 91.6 us; the launch traced here: 91.3 us
  waiting for transfers between devices  23.4 us (26%)
  starting transfers between devices  15.7 us (17%)
  between operations  13.7 us (15%)
  matrix products  13.4 us (15%)
  blocking collectives  13.3 us (15%)
  local copies, waits for them, and re-layouts  7.98 us (9%)
  other arithmetic  3.78 us (4%)
    reduce_scatter x1, waiting for transfers between devices, on_device(): lax.psum_scatter(phi_sum(cos_table, sin_table, coef), 'strip', scatter_di...  16.3 us
    all_to_all x1, blocking collectives, on_device(): lax.all_to_all(values, ('strip', 'mr'), split_axis=0, concat_axis=0, tile...  13.3 us
    dot_general x1, matrix products, on_device(): jnp.einsum('cmkl,mkrl->cmkr', mixed, wigner, preferred_element_type=jnp.f...  6.85 us
    ppermute x2, starting transfers between devices, padded_2(): after = lax.ppermute(first, axis, down)  6.45 us
    all_to_all x1, starting transfers between devices, on_device(): coef = lax.all_to_all(coef, 'mr', split_axis=3, concat_axis=1, tiled=True)  5.17 us
    all_to_all x1, starting transfers between devices, on_device(): lax.all_to_all(packet, ('strip', 'mr'), split_axis=1, concat_axis=1, tile...  3.97 us
    all_to_all x1, waiting for transfers between devices, on_device(): coef = lax.all_to_all(coef, 'mr', split_axis=3, concat_axis=1, tiled=True)  3.3 us
    ppermute x2, waiting for transfers between devices, padded_2(): before = lax.ppermute(last, axis, up)  2.75 us
  transfers between devices with their start and end apart: 7, of which 5 were waited for; matrix products, arithmetic and copies ran while one was open for 14% of the time, Pallas kernels for 0%

commit v1 on v0

--- a/solution.py
+++ b/solution.py
@@ -136,7 +136,15 @@
         [weights, base_index.reshape(1, devices, cap).astype(jnp.float32)], axis=0
     )
     values = owner_values(
-        lax.all_to_all(packet, ("strip", "mr"), split_axis=1, concat_axis=1, tiled=True),
+        jnp.concatenate(
+            lax.all_to_all(
+                jnp.stack(jnp.split(packet, lax.axis_size(("strip", "mr")), axis=1)),
+                ("strip", "mr"),
+                0,
+                0,
+            ),
+            axis=1,
+        ),
         padded,
         lat_dev,
         phi_dev,

time: 91.6 us -> 111 us (1.21)
  local copies, waits for them, and re-layouts: 7.98 us -> 28.6 us
  waiting for transfers between devices: 23.4 us -> 20.1 us
  starting transfers between devices: 15.7 us -> 18 us
    unnamed x8 -> x39, local copies, waits for them, and re-layouts: 1.11 us -> 19.4 us
    all_to_all x1, waiting for transfers between devices: 3.3 us -> 0.01 us  [on_device(): coef = lax.all_to_all(coef, 'mr', split_axis=3, concat_axis=1, tiled=True)]
    split x0 -> x34, local copies, waits for them, and re-layouts: none -> 2.66 us  [on_device(): jnp.split(packet, lax.axis_size(('strip', 'mr')), axis=1)]
    all_to_all x1, starting transfers between devices: 3.97 us -> 6.32 us  [on_device(): lax.all_to_all(jnp.stack(jnp.split(packet, lax.axis_size(('strip', 'mr'))...]
  transfers between devices with their start and end apart: 7 -> 7, of which waited for: 5 -> 4; matrix products, arithmetic and copies ran while one was open for 14% -> 30% of each run, Pallas kernels for 0% -> 0%
where the time goes in v1:
time: 111 us
  local copies, waits for them, and re-layouts  28.6 us (26%)
  waiting for transfers between devices  20.1 us (18%)
  starting transfers between devices  18 us (16%)
  between operations  13.8 us (12%)
  matrix products  13.4 us (12%)
  blocking collectives  13.2 us (12%)
  other arithmetic  3.78 us (3%)
    unnamed x39, local copies, waits for them, and re-layouts  19.4 us
    reduce_scatter x1, waiting for transfers between devices, on_device(): lax.psum_scatter(phi_sum(cos_table, sin_table, coef), 'strip', scatter_di...  16.3 us
    all_to_all x1, blocking collectives, on_device(): lax.all_to_all(values, ('strip', 'mr'), split_axis=0, concat_axis=0, tile...  13.2 us
    dot_general x1, matrix products, on_device(): jnp.einsum('cmkl,mkrl->cmkr', mixed, wigner, preferred_element_type=jnp.f...  6.85 us
    ppermute x2, starting transfers between devices, padded_2(): after = lax.ppermute(first, axis, down)  6.45 us
    all_to_all x1, starting transfers between devices, on_device(): lax.all_to_all(jnp.stack(jnp.split(packet, lax.axis_size(('strip', 'mr'))...  6.32 us
    all_to_all x1, starting transfers between devices, on_device(): coef = lax.all_to_all(coef, 'mr', split_axis=3, concat_axis=1, tiled=True)  5.17 us
    ppermute x2, waiting for transfers between devices, padded_2(): before = lax.ppermute(last, axis, up)  2.75 us
  transfers between devices with their start and end apart: 7, of which 4 were waited for; matrix products, arithmetic and copies ran while one was open for 30% of the time, Pallas kernels for 0%

profile of v1, /device:TPU:0, one launch (start us, length us, event | category | flops | bytes accessed | tf_op | source)
XLA Modules:
  0.0 111.0 jit_solution(15138845396851755852)
XLA Ops:
  6.5 1.0 copy.351
  7.5 6.8 %fusion.2 = bf16[2,8,13,32]{3,0,2,1:T(2,128)(2,1)S(1)} fusion(bf16[8,13,32,2048]{3,2,1,0:T(8,128)(2,1)} %param.8, f32[13,2048]{1,0:T(8,128)} %param.7, f32[2,8,2048]{2,0,1:T(2,128)S(1)} %copy.351), kind=kOutput, calls=%fused_computation.8 | convolution fusion | flops 28121600 | bytes 13882368 | tf_op jit(solution)/shard_map/cmkl,mkrl->cmkr/dot_general | solution.py:97
  14.6 0.8 reshape.389
  15.4 5.2 %all-to-all-start = ((bf16[8,2,416]{2,1,0:T(2,128)(2,1)}), bf16[8,2,416]{2,1,0:T(2,128)(2,1)S(1)}, u32[]{:S(2)}, u32[]{:S(2)}) async-start(bf16[8,2,416]{2,1,0:T(2,128)(2,1)} %reshape.389), calls=%async_computation | async-start | bytes 32768 | tf_op jit(solution)/shard_map/all_to_all | solution.py:100
  24.3 0.6 constant_dynamic-update-slice_fusion.30
  26.7 0.6 constant_dynamic-update-slice_fusion.26
  29.7 0.6 constant_dynamic-update-slice_fusion.21
  33.2 0.6 constant_dynamic-update-slice_fusion.15
  35.6 0.6 constant_dynamic-update-slice_fusion.11
  39.1 0.6 constant_dynamic-update-slice_fusion.5
  39.7 0.6 constant_dynamic-update-slice_fusion.4
  41.5 0.6 constant_dynamic-update-slice_fusion.1
  42.1 0.6 constant_dynamic-update-slice_fusion
  42.7 6.3 %all-to-all-start.1 = ((f32[32,13,1,8]{1,3,2,0:T(8,128)}), f32[32,13,1,8]{1,3,2,0:T(8,128)S(1)}, u32[]{:S(2)}, u32[]{:S(2)}) async-start(f32[32,13,1,8]{1,3,2,0:T(8,128)} %constant_dynamic-update-slice_fusion), calls=%async_computation.2 | async-start | bytes 262144 | tf_op jit(solution)/shard_map/all_to_all | solution.py:140
  49.9 1.3 %fusion.22 = f32[512,52]{0,1:T(8,128)S(1)} fusion(bf16[64,52]{0,1:T(8,128)(2,1)S(1)} %squeeze.4, s32[64]{0:T(128)S(1)} %iota_add_fusion.2), kind=kOutput, calls=%fused_computation.55 | convolution fusion | flops 3899392 | bytes 113408 | tf_op jit(solution)/shard_map/dot_general | solution.py:43
  51.2 1.3 %fusion.21 = f32[512,52]{0,1:T(8,128)S(1)} fusion(bf16[64,52]{0,1:T(8,128)(2,1)S(1)} %squeeze.4, s32[64]{0:T(128)S(1)} %iota_add_fusion.2), kind=kOutput, calls=%fused_computation.54 | convolution fusion | flops 3899392 | bytes 113408 | tf_op jit(solution)/shard_map/dot_general | solution.py:40
  52.9 1.3 %convolution_add_fusion = f32[512,52]{0,1:T(8,128)S(1)} fusion(f32[512,52]{0,1:T(8,128)S(1)} %fusion.22, bf16[64,52]{0,1:T(8,128)(2,1)S(1)} %squeeze.10, s32[64]{0:T(128)S(1)} %iota_add_fusion.2), kind=kOutput, calls=%fused_computation.3 | convolution fusion | flops 3926016 | bytes 219904 | tf_op jit(solution)/shard_map/dot_general | solution.py:43
  54.2 1.3 %convolution_subtract_fusion = f32[512,52]{0,1:T(8,128)S(1)} fusion(f32[512,52]{0,1:T(8,128)S(1)} %fusion.21, bf16[64,52]{0,1:T(8,128)(2,1)S(1)} %squeeze.10, s32[64]{0:T(128)S(1)} %iota_add_fusion.2), kind=kOutput, calls=%fused_computation.4 | convolution fusion | flops 3926016 | bytes 219904 | tf_op jit(solution)/shard_map/dot_general | solution.py:40
  55.5 0.7 pad_maximum_fusion
  56.2 1.0 all-to-all-done.1
  57.2 0.7 fusion.23
  57.9 1.2 %remainder_reduce_fusion = (s32[32,8]{1,0:T(8,128)S(1)}, s32[32,8]{1,0:T(8,128)S(1)}) fusion(f32[13,32,1,8]{0,3,2,1:T(8,128)S(1)} %bitcast.118), kind=kLoop, calls=%fused_computation.53 | loop fusion | flops 768 | bytes 3072 | tf_op jit(solution)/shard_map/jit(remainder)/rem | solution.py:50
  59.2 0.9 slice_reduce_fusion.3
  60.8 16.3 %reduce-scatter.2.cloned.1.call-done = f32[128,104]{0,1:T(8,128)} async-done(((f32[512,104]{0,1:T(8,128)}), f32[128,104]{0,1:T(8,128)}) %reduce-scatter.2.cloned.1.call-update) | async-done | bytes 53264 | tf_op jit(solution)/shard_map/reduce_scatter | solution.py:112
  77.1 1.1 fusion.4
  78.3 3.8 %collective-permute-start.1 = (bf16[25,4,2]{2,0,1:T(8,128)(2,1)S(1)}, bf16[25,4,2]{2,0,1:T(8,128)(2,1)S(1)}, u32[]{:S(2)}, u32[]{:S(2)}) collective-permute-start(bf16[25,4,2]{2,0,1:T(8,128)(2,1)S(1)} %get-tuple-element.56), channel_id=1, source_target_pairs={{8,0},{16,8},{24,16},{0,24},{9,1},{17,9},{25,17},{1,25},{10,2},{18... | collective-permute-start | bytes 1208 | tf_op jit(solution)/shard_map/ppermute | solution.py:16
  82.1 1.9 %collective-permute-done = bf16[25,4,2]{2,0,1:T(8,128)(2,1)S(1)} collective-permute-done((bf16[25,4,2]{2,0,1:T(8,128)(2,1)S(1)}, bf16[25,4,2]{2,0,1:T(8,128)(2,1)S(1)}, u32[]{:S(2)}, u32[]{:S(2)}) %collective-permute-start) | collective-permute-done | bytes 432 | tf_op jit(solution)/shard_map/ppermute | solution.py:15
  84.2 2.6 %collective-permute-start.3 = (bf16[25,2,132]{2,0,1:T(8,128)(2,1)S(1)}, bf16[25,2,132]{2,0,1:T(8,128)(2,1)S(1)}, u32[]{:S(2)}, u32[]{:S(2)}) collective-permute-start(bf16[25,2,132]{2,0,1:T(8,128)(2,1)S(1)} %get-tuple-element.54), channel_id=1, source_target_pairs={{1,0},{2,1},{3,2},{4,3},{5,4},{6,5},{7,6},{0,7},{9,8},{10,9},{11,1... | collective-permute-start | bytes 39608 | tf_op jit(solution)/shard_map/ppermute | solution.py:16
  87.5 0.9 collective-permute-done.2
  89.0 13.2 %all_to_all.29 = f32[32,1,8]{2,1,0:T(1,128)S(1)} all-to-all(f32[32,1,8]{2,1,0:T(1,128)S(1)} %bitcast.124), channel_id=1, replica_groups=mesh['strip'=4,'mr'=8] {'strip','mr'}, dimensions={0} | all-to-all | bytes 2048 | tf_op jit(solution)/shard_map/all_to_all | solution.py:153
  102.8 0.7 reduce.33
  103.5 0.7 reshape.361
  (120 shorter events, 20.9 us)
Async XLA Ops:
  6.5 14.0 %copy-start = (f32[12,256]{1,0:T(8,128)S(1)}, f32[12,256]{1,0:T(8,128)}, u32[]{:S(2)}) copy-start(f32[12,256]{1,0:T(8,128)} %param.10) | copy-start | bytes 36868
  6.5 14.3 %slice-start = ((f32[12,256]{1,0:T(8,128)}), f32[4,256]{1,0:T(4,128)S(1)}, s32[]{:S(2)}) async-start(f32[12,256]{1,0:T(8,128)} %param.10), calls=%async_computation.5 | async-start | bytes 8192 | tf_op jit(solution)/shard_map/slice | solution.py:132
  6.5 14.1 %copy-start.1 = (s32[256]{0:T(256)S(1)}, s32[256]{0:T(256)}, u32[]{:S(2)}) copy-start(s32[256]{0:T(256)} %param.9) | copy-start | bytes 3076
  6.5 14.2 %copy-start.2 = (s32[1,32]{1,0:T(1,128)S(1)}, s32[1,32]{1,0:T(1,128)}, u32[]{:S(2)}) copy-start(s32[1,32]{1,0:T(1,128)} %param.11) | copy-start | bytes 388
  15.4 27.3 %all-to-all-start = ((bf16[8,2,416]{2,1,0:T(2,128)(2,1)}), bf16[8,2,416]{2,1,0:T(2,128)(2,1)S(1)}, u32[]{:S(2)}, u32[]{:S(2)}) async-start(bf16[8,2,416]{2,1,0:T(2,128)(2,1)} %reshape.389), calls=%async_computation | async-start | bytes 32768 | tf_op jit(solution)/shard_map/all_to_all | solution.py:100
  42.7 14.6 %all-to-all-start.1 = ((f32[32,13,1,8]{1,3,2,0:T(8,128)}), f32[32,13,1,8]{1,3,2,0:T(8,128)S(1)}, u32[]{:S(2)}, u32[]{:S(2)}) async-start(f32[32,13,1,8]{1,3,2,0:T(8,128)} %constant_dynamic-update-slice_fusion), calls=%async_computation.2 | async-start | bytes 262144 | tf_op jit(solution)/shard_map/all_to_all | solution.py:140
  49.0 28.1 %reduce-scatter.2.cloned.1.call-start = ((), (), s32[]{:S(2)}) async-start(), calls=%async_computation.4 | async-start | bytes 266240 | tf_op jit(solution)/shard_map/reduce_scatter | solution.py:112
  78.3 5.7 %collective-permute-start = (bf16[25,4,2]{2,0,1:T(8,128)(2,1)S(1)}, bf16[25,4,2]{2,0,1:T(8,128)(2,1)S(1)}, u32[]{:S(2)}, u32[]{:S(2)}) collective-permute-start(bf16[25,4,2]{2,0,1:T(8,128)(2,1)S(1)} %get-tuple-element.55), channel_id=1, source_target_pairs={{0,8},{8,16},{16,24},{24,0},{1,9},{9,17},{17,25},{25,1},{2,10},{10... | collective-permute-start | bytes 1208 | tf_op jit(solution)/shard_map/ppermute | solution.py:15
  78.3 5.7 %collective-permute-start.1 = (bf16[25,4,2]{2,0,1:T(8,128)(2,1)S(1)}, bf16[25,4,2]{2,0,1:T(8,128)(2,1)S(1)}, u32[]{:S(2)}, u32[]{:S(2)}) collective-permute-start(bf16[25,4,2]{2,0,1:T(8,128)(2,1)S(1)} %get-tuple-element.56), channel_id=1, source_target_pairs={{8,0},{16,8},{24,16},{0,24},{9,1},{17,9},{25,17},{1,25},{10,2},{18... | collective-permute-start | bytes 1208 | tf_op jit(solution)/shard_map/ppermute | solution.py:16
  84.1 4.3 %collective-permute-start.2 = (bf16[25,2,132]{2,0,1:T(8,128)(2,1)S(1)}, bf16[25,2,132]{2,0,1:T(8,128)(2,1)S(1)}, u32[]{:S(2)}, u32[]{:S(2)}) collective-permute-start(bf16[25,2,132]{2,0,1:T(8,128)(2,1)S(1)} %get-tuple-element.53), channel_id=1, source_target_pairs={{0,1},{1,2},{2,3},{3,4},{4,5},{5,6},{6,7},{7,0},{8,9},{9,10},{10,1... | collective-permute-start | bytes 39608 | tf_op jit(solution)/shard_map/ppermute | solution.py:15
  84.2 4.2 %collective-permute-start.3 = (bf16[25,2,132]{2,0,1:T(8,128)(2,1)S(1)}, bf16[25,2,132]{2,0,1:T(8,128)(2,1)S(1)}, u32[]{:S(2)}, u32[]{:S(2)}) collective-permute-start(bf16[25,2,132]{2,0,1:T(8,128)(2,1)S(1)} %get-tuple-element.54), channel_id=1, source_target_pairs={{1,0},{2,1},{3,2},{4,3},{5,4},{6,5},{7,6},{0,7},{9,8},{10,9},{11,1... | collective-permute-start | bytes 39608 | tf_op jit(solution)/shard_map/ppermute | solution.py:16
Sparse Core Ops, SparseCore 0:
  56.3 20.7 reduce-scatter.1
